TPU v7x, 32 devices: a whole 2x2x4 slice. The times are simulated.
32 devices in a mesh: ctx: 8 (over y, x, core), ch: 4 (over z).
Axes of the slice: x: 2, y: 2, z: 4, core: 2. Of those that a mesh axis runs over, the one named last changes fastest.
Arguments:
- query_act: bfloat16 [4096, 4096], P('ctx', 'ch'), may hold values from -6 to 6
- key_act: bfloat16 [4096, 4096], P('ctx', 'ch'), may hold values from -6 to 6
- value_act: bfloat16 [4096, 4096], P('ctx', 'ch'), may hold values from -6 to 6
- filters: bfloat16 [4096, 128], P('ch'), may hold values from -0.5 to 0.5
- proj_weight: bfloat16 [8192, 4096], P('ctx', 'ch'), may hold values from -0.09375 to 0.09375
- cotangent: bfloat16 [4096, 8192], P('ctx', 'ch'), may hold values from -6 to 6
Outputs:
- grad_query: bfloat16 [4096, 4096], P('ctx', 'ch')
- grad_key: bfloat16 [4096, 4096], P('ctx', 'ch')
- grad_value: bfloat16 [4096, 4096], P('ctx', 'ch')
- grad_filter: float32 [4096, 128], P('ch')
- grad_proj: float32 [8192, 4096], P('ctx', 'ch')
All inputs are finite; a program needn't handle non-finite values.
Results may differ from a plain program's by a relative error of at most 0.0051.
Values may be sent and summed in bfloat16 or wider, within the bound.
A program may use at most 192 MiB of HBM per device.

v0:
```python
import jax
import jax.numpy as jnp
from jax import lax
from jax.sharding import PartitionSpec as P

TAPS = 128


def from_behind(x, axis, by):
    length = lax.axis_size(axis)
    pairs = [(i, i + by) for i in range(length) if 0 <= i + by < length]
    return lax.ppermute(x, axis, pairs)


def tap_sum(filt_f, extended, tokens, causal):
    group_width = 8
    group_count = TAPS // group_width
    channels = extended.shape[1]

    def tap_one_group(group_index, total):
        group_start = group_index.astype(jnp.int32) * group_width
        if causal:
            first = jnp.int32(TAPS - group_width) - group_start
        else:
            first = group_start
        slab = lax.dynamic_slice_in_dim(extended, first, tokens + group_width - 1, 0).astype(
            jnp.float32
        )
        weights = lax.dynamic_slice_in_dim(filt_f, group_start, group_width, 1)
        for inner in range(group_width):
            if causal:
                begin = group_width - 1 - inner
            else:
                begin = inner
            total = total + weights[:, inner][None, :] * slab[begin : begin + tokens]
        return total

    return lax.fori_loop(0, group_count, tap_one_group, jnp.zeros((tokens, channels), jnp.float32))


def filter_sums(grad_gate, lagged):
    tokens = grad_gate.shape[0]
    group_width = 8
    group_count = TAPS // group_width
    gate_f = grad_gate.astype(jnp.float32)

    def filter_one_group(group_index):
        first = jnp.int32(TAPS - group_width) - group_index * group_width
        lag_slab = lax.dynamic_slice_in_dim(lagged, first, tokens + group_width - 1, 0).astype(
            jnp.float32
        )
        stacked = jnp.stack(
            [
                lag_slab[group_width - 1 - inner : group_width - 1 - inner + tokens]
                for inner in range(group_width)
            ],
            0,
        )
        return jnp.sum(stacked * gate_f[None], axis=1)

    sums = lax.map(filter_one_group, jnp.arange(group_count, dtype=jnp.int32))
    return sums.reshape(TAPS, grad_gate.shape[1]).T


def shards(query_act, key_act, value_act, filters, proj_weight, cotangent):
    tokens = query_act.shape[0]
    gathered = lax.all_gather(cotangent, "ch", axis=1, tiled=True)
    query_f = query_act.astype(jnp.float32)
    key_f = key_act.astype(jnp.float32)
    value_f = value_act.astype(jnp.float32)
    filt_f = filters.astype(jnp.float32)
    product = (key_f * value_f).astype(jnp.bfloat16)
    before = from_behind(product[tokens - TAPS + 1 :], "ctx", 1)
    lagged = jnp.concatenate([before, product], 0)
    mixed = tap_sum(filt_f, lagged, tokens, True)
    gated = (query_f * mixed).astype(jnp.bfloat16)
    grad_mix = jnp.dot(
        gathered,
        lax.all_gather(proj_weight, "ctx", axis=0, tiled=True),
        preferred_element_type=jnp.float32,
    )
    grad_query = (grad_mix * mixed).astype(jnp.bfloat16)
    grad_gate = (grad_mix * query_f).astype(jnp.bfloat16)
    after = from_behind(grad_gate[: TAPS - 1], "ctx", -1)
    leading = jnp.concatenate([grad_gate, after], 0)
    grad_prod = tap_sum(filt_f, leading, tokens, False)
    grad_key = (grad_prod * value_f).astype(jnp.bfloat16)
    grad_value = (grad_prod * key_f).astype(jnp.bfloat16)
    local_filter = filter_sums(grad_gate, lagged)
    grad_filter = lax.psum(local_filter, "ctx")
    own_rows = proj_weight.shape[0]
    partial_grad = lax.dot_general(
        gathered, gated, (((0,), (0,)), ((), ())), preferred_element_type=jnp.float32
    )
    summed = lax.psum(partial_grad, "ctx")
    grad_proj = lax.dynamic_slice_in_dim(summed, lax.axis_index("ctx") * own_rows, own_rows, 0)
    return (grad_query, grad_key, grad_value, grad_filter, grad_proj)


def solution(mesh):
    return jax.shard_map(
        shards,
        mesh=mesh,
        in_specs=(
            P("ctx", "ch"),
            P("ctx", "ch"),
            P("ctx", "ch"),
            P("ch", None),
            P("ctx", "ch"),
            P("ctx", "ch"),
        ),
        out_specs=(P("ctx", "ch"), P("ctx", "ch"), P("ctx", "ch"), P("ch", None), P("ctx", "ch")),
        check_vma=False,
    )
```

profile of v0, /device:TPU:0, one launch (start us, length us, event | category | flops | bytes accessed | tf_op | source)
XLA Modules:
  0.0 1226.1 jit_solution(14841337921941511170)
XLA Ops:
  8.7 153.2 %all-gather.3.cloned.1.call-done = bf16[512,8192]{1,0:T(8,128)(2,1)} async-done(((bf16[512,2048]{1,0:T(8,128)(2,1)}), bf16[512,8192]{1,0:T(8,128)(2,1)}) %all-gather.3.cloned.1.call-update) | async-done | bytes 8388624 | tf_op jit(solution)/shard_map/all_gather | solution.py:67
  162.0 90.0 %all-gather.5.cloned.1.call-done = bf16[8192,1024]{1,0:T(8,128)(2,1)} async-done(((bf16[1024,1024]{1,0:T(8,128)(2,1)}), bf16[8192,1024]{1,0:T(8,128)(2,1)}) %all-gather.5.cloned.1.call-update) | async-done | bytes 16777232 | tf_op jit(solution)/shard_map/all_gather | solution.py:79
  251.9 16.1 %fusion.30 = (f32[512,1024]{1,0:T(8,128)}, bf16[512,1024]{1,0:T(8,128)(2,1)S(1)}, f32[512,1024]{1,0:T(8,128)}) fusion(bf16[512,1024]{1,0:T(8,128)(2,1)S(1)} %copy-done.2, bf16[512,8192]{1,0:T(8,128)(2,1)} %all-gather.3.cloned.1.call-done, bf16[8192,1024]{1,0:T(8,128)(2,1)} %all-gather.5.cloned.1.call-done), kind=kOutput, calls=%fused_computation.84 | convolution fusion | flops 8592031744 | bytes 31457280 | tf_op jit(solution)/shard_map/dot_general | solution.py:77
  271.6 90.8 %while.44 = (s32[]{:T(128)}, f32[512,1024]{1,0:T(8,128)}, f32[1024,128]{0,1:T(8,128)}, bf16[639,1024]{1,0:T(8,128)(2,1)S(1)}, s32[]{:T(128)}, /*index=5*/s32[]{:...) while((s32[]{:T(128)}, f32[512,1024]{1,0:T(8,128)}, ...), condition=%wide.region_3.0_spmd.clone, body=%wide.region_2.0_spmd.clone.sunk | while | flops 9444368 | bytes 24258916 | solution.py:38
  366.8 6.6 collective-permute-start
  374.6 91.0 %while.43 = (s32[]{:T(128)}, f32[512,1024]{1,0:T(8,128)}, f32[1024,128]{0,1:T(8,128)}, bf16[639,1024]{1,0:T(8,128)(2,1)S(1)}, s32[]{:T(128)}, /*index=5*/s32[]{:...) while((s32[]{:T(128)}, f32[512,1024]{1,0:T(8,128)}, ...), condition=%wide.region_1.0_spmd.clone, body=%wide.region_0.0_spmd.clone.sunk | while | flops 9444370 | bytes 24258944 | solution.py:38
  380.6 4.4 fusion.53
  386.4 4.4 fusion.53
  403.7 4.4 fusion.53
  409.6 4.4 fusion.53
  438.2 4.4 fusion.53
  465.7 315.1 %while.42 = (s32[]{:T(128)}, f32[16,8,1024]{2,1,0:T(8,128)}, s32[16]{0:T(128)S(1)}, bf16[639,1024]{1,0:T(8,128)(2,1)S(1)}, f32[512,1024]{1,0:T(8,128)}, /*index=...) while((s32[]{:T(128)}, f32[16,8,1024]{2,1,0:T(8,128)}, s32[16]{0:T(128)S(1)}, ...), condition=%wide.region_6.7_spmd, body=%wide.region_4.6_spmd.sunk | while | flops 8911879 | bytes 122824920 | solution.py:61
  470.3 5.7 copy-done
  476.0 8.8 multiply_reduce_fusion.2
  489.9 5.7 copy-done
  495.7 8.8 multiply_reduce_fusion.2
  509.6 5.7 copy-done
  515.4 8.8 multiply_reduce_fusion.2
  529.3 5.7 copy-done
  535.0 8.8 multiply_reduce_fusion.2
  549.0 5.7 copy-done
  554.7 8.8 multiply_reduce_fusion.2
  568.7 5.7 copy-done
  574.4 8.8 multiply_reduce_fusion.2
  588.4 5.7 copy-done
  594.1 8.8 multiply_reduce_fusion.2
  608.1 5.7 copy-done
  613.8 8.8 multiply_reduce_fusion.2
  627.8 5.7 copy-done
  633.5 8.8 multiply_reduce_fusion.2
  647.4 5.7 copy-done
  653.2 8.8 multiply_reduce_fusion.2
  667.1 5.7 copy-done
  672.9 8.8 multiply_reduce_fusion.2
  686.8 5.7 copy-done
  692.6 8.8 multiply_reduce_fusion.2
  706.5 5.7 copy-done
  712.2 8.8 multiply_reduce_fusion.2
  726.2 5.7 copy-done
  731.9 8.8 multiply_reduce_fusion.2
  745.9 5.7 copy-done
  751.6 8.8 multiply_reduce_fusion.2
  765.6 5.7 copy-done
  771.3 8.8 multiply_reduce_fusion.2
  780.7 17.9 %convolution_bitcast_fusion = f32[8192,1024]{0,1:T(8,128)} fusion(bf16[512,8192]{1,0:T(8,128)(2,1)} %all-gather.3.cloned.1.call-done, f32[512,1024]{1,0:T(8,128)S(1)} %copy-done.1, bf16[512,1024]{1,0:T(8,128)(2,1)} %param.12), kind=kOutput, calls=%fused_computation.69 | convolution fusion | flops 8591507456 | bytes 45088768 | tf_op jit(solution)/shard_map/dot_general | solution.py:92
  801.5 405.9 %all-reduce.3.cloned.1.call-done = (f32[1024,128]{0,1:T(8,128)}, f32[8192,1024]{0,1:T(8,128)}) async-done(((f32[1024,128]{0,1:T(8,128)}, f32[8192,1024]{0,1:T(8,128)}), (f32[1024,128]{0,1:T(8,128)}, f32[8192,1024]{0,1:T(8,128)})) %all-reduce.3.cloned.1.call-update) | async-done | bytes 34078736 | tf_op jit(solution)/shard_map/psum | solution.py:90
  1209.4 4.9 constant_dynamic-slice_fusion.16
  1214.3 5.3 copy.15
  (311 shorter events, 245.2 us)
Async XLA Ops:
  7.2 244.8 %copy-start.2 = (bf16[512,1024]{1,0:T(8,128)(2,1)S(1)}, bf16[512,1024]{1,0:T(8,128)(2,1)}, u32[]{:S(2)}) copy-start(bf16[512,1024]{1,0:T(8,128)(2,1)} %param.12) | copy-start | bytes 3145732
  7.2 154.8 %all-gather.3.cloned.1.call-start = ((), (), s32[]{:S(2)}) async-start(), calls=%async_computation | async-start | bytes 10485760 | tf_op jit(solution)/shard_map/all_gather | solution.py:67
  7.9 244.0 %all-gather.5.cloned.1.call-start = ((), (), s32[]{:S(2)}) async-start(), calls=%async_computation.1 | async-start | bytes 18874368 | tf_op jit(solution)/shard_map/all_gather | solution.py:79
  8.7 260.7 %copy-start.3 = (bf16[1024,128]{1,0:T(8,128)(2,1)S(1)}, bf16[1024,128]{1,0:T(8,128)(2,1)}, u32[]{:S(2)}) copy-start(bf16[1024,128]{1,0:T(8,128)(2,1)} %param.15) | copy-start | bytes 786436
  8.7 1198.7 %all-reduce.3.cloned.1.call-start = ((), (), s32[]{:S(2)}) async-start(), calls=%async_computation.2 | async-start | bytes 68157440 | tf_op jit(solution)/shard_map/psum | solution.py:90
  268.1 3.4 collective-permute-start.1
  366.8 7.6 collective-permute-start
  465.7 315.1 %copy-start.1 = (f32[512,1024]{1,0:T(8,128)S(1)}, f32[512,1024]{1,0:T(8,128)}, u32[]{:S(2)}) copy-start(f32[512,1024]{1,0:T(8,128)} %get-tuple-element.259) | copy-start | bytes 6291460
  470.2 5.8 copy-start
  489.9 5.8 copy-start
  509.6 5.8 copy-start
  529.3 5.8 copy-start
  549.0 5.8 copy-start
  568.7 5.8 copy-start
  588.4 5.8 copy-start
  608.1 5.8 copy-start
  627.7 5.8 copy-start
  647.4 5.8 copy-start
  667.1 5.8 copy-start
  686.8 5.8 copy-start
  706.5 5.8 copy-start
  726.2 5.8 copy-start
  745.9 5.8 copy-start
  765.6 5.8 copy-start
Sparse Core Ops, SparseCore 0:
  9.6 152.3 all-gather.2
  163.8 88.0 all-gather.4
  798.7 408.6 all-reduce.2
where the time goes:
time: 1230 us
  waiting for transfers between devices  653 us (53%)
  other arithmetic  299 us (24%)
  local copies, waits for them, and re-layouts  206 us (17%)
  matrix products  34 us (3%)
  between operations  13.9 us (1%)
  loops' own time  12.8 us (1%)
    psum x1, waiting for transfers between devices, shards(): grad_filter = lax.psum(local_filter, 'ctx')  406 us
    all_gather x1, waiting for transfers between devices, shards(): gathered = lax.all_gather(cotangent, 'ch', axis=1, tiled=True)  153 us
    reduce_sum x16, other arithmetic, filter_one_group(): return jnp.sum(stacked * gate_f[None], axis=1)  141 us
    add x32, other arithmetic, tap_one_group(): total = total + weights[:, inner][None, :] * slab[begin:begin + tokens]  137 us
    while x144, local copies, waits for them, and re-layouts  135 us
    all_gather x1, waiting for transfers between devices, shards(): lax.all_gather(proj_weight, 'ctx', axis=0, tiled=True)  90 us
    slice x32, local copies, waits for them, and re-layouts, tap_one_group(): total = total + weights[:, inner][None, :] * slab[begin:begin + tokens]  35.9 us
  transfers between devices with their start and end apart: 5, of which 5 were waited for; matrix products, arithmetic and copies ran while one was open for 0% of the time, Pallas kernels for 0%

commit v1 on v0

--- a/solution.py
+++ b/solution.py
@@ -64,7 +64,16 @@
 
 def shards(query_act, key_act, value_act, filters, proj_weight, cotangent):
     tokens = query_act.shape[0]
-    gathered = lax.all_gather(cotangent, "ch", axis=1, tiled=True)
+    ways = lax.axis_size("ch")
+    up = [(d, (d + 1) % ways) for d in range(ways)]
+    down = [(d, (d - 1) % ways) for d in range(ways)]
+    earlier, later = ([cotangent], [cotangent])
+    for _ in range(ways // 2):
+        earlier.append(lax.ppermute(earlier[-1], "ch", up))
+    for _ in range((ways - 1) // 2):
+        later.append(lax.ppermute(later[-1], "ch", down))
+    line = jnp.concatenate([*earlier[::-1], *later[1:]], axis=1)
+    gathered = jnp.roll(line, (lax.axis_index("ch") - ways // 2) * cotangent.shape[1], axis=1)
     query_f = query_act.astype(jnp.float32)
     key_f = key_act.astype(jnp.float32)
     value_f = value_act.astype(jnp.float32)

time: 1230 us -> 1130 us (0.919)
  waiting for transfers between devices: 653 us -> 535 us
  local copies, waits for them, and re-layouts: 206 us -> 286 us
  other arithmetic: 299 us -> 235 us
    all_gather x1 -> x0, waiting for transfers between devices: 153 us -> none  [shards(): gathered = lax.all_gather(cotangent, 'ch', axis=1, tiled=True)]
    ppermute x0 -> x3, waiting for transfers between devices: none -> 128 us  [the longest x2 94.6 us: shards(): earlier.append(lax.ppermute(earlier[-1], 'ch', up))]
    all_gather x1, waiting for transfers between devices: 90 us -> 0.01 us  [shards(): lax.all_gather(proj_weight, 'ctx', axis=0, tiled=True)]
    add x32, other arithmetic: 137 us -> 71 us  [tap_one_group(): total = total + weights[:, inner][None, :] * slab[begin:begin + tokens]]
    while x144 -> x112, local copies, waits for them, and re-layouts: 135 us -> 176 us
    another operation x16, local copies, waits for them, and re-layouts: 3.88 us -> 22.9 us  [filter_one_group(): jnp.stack([lag_slab[group_width - 1 - inner:group_width - 1 - inner + tok...]
    unnamed x9 -> x19, local copies, waits for them, and re-layouts: 7.53 us -> 23.3 us
  transfers between devices with their start and end apart: 5 -> 7, of which waited for: 5 -> 6; matrix products, arithmetic and copies ran while one was open for 0% -> 2% of each run, Pallas kernels for 0% -> 0%
where the time goes in v1:
time: 1130 us
  waiting for transfers between devices  535 us (47%)
  local copies, waits for them, and re-layouts  286 us (25%)
  other arithmetic  235 us (21%)
  matrix products  34 us (3%)
  starting transfers between devices  14.7 us (1%)
  between operations  14.1 us (1%)
  loops' own time  12.3 us (1%)
    psum x1, waiting for transfers between devices, shards(): grad_filter = lax.psum(local_filter, 'ctx')  404 us
    while x112, local copies, waits for them, and re-layouts  176 us
    reduce_sum x16, other arithmetic, filter_one_group(): return jnp.sum(stacked * gate_f[None], axis=1)  141 us
    ppermute x2, waiting for transfers between devices, shards(): earlier.append(lax.ppermute(earlier[-1], 'ch', up))  94.6 us
    add x32, other arithmetic, tap_one_group(): total = total + weights[:, inner][None, :] * slab[begin:begin + tokens]  71 us
    slice x32, local copies, waits for them, and re-layouts, tap_one_group(): total = total + weights[:, inner][None, :] * slab[begin:begin + tokens]  35.9 us
    ppermute x1, waiting for transfers between devices, shards(): later.append(lax.ppermute(later[-1], 'ch', down))  33.6 us
    unnamed x19, local copies, waits for them, and re-layouts  23.3 us
  transfers between devices with their start and end apart: 7, of which 6 were waited for; matrix products, arithmetic and copies ran while one was open for 2% of the time, Pallas kernels for 0%

profile of v1, /device:TPU:0, one launch (start us, length us, event | category | flops | bytes accessed | tf_op | source)
XLA Modules:
  0.0 1131.1 jit_solution(8232195062178722568)
XLA Ops:
  8.8 3.0 collective-permute-start
  11.8 47.8 %collective-permute-done = bf16[512,2048]{1,0:T(8,128)(2,1)} collective-permute-done((bf16[512,2048]{1,0:T(8,128)(2,1)S(1)}, bf16[512,2048]{1,0:T(8,128)(2,1)}, u32[]{:S(2)}, u32[]{:S(2)}) %collective-permute-start) | collective-permute-done | bytes 2097184 | tf_op jit(solution)/shard_map/ppermute | solution.py:72
  59.5 3.8 collective-permute-start.2
  63.4 46.9 %collective-permute-done.1 = bf16[512,2048]{1,0:T(8,128)(2,1)} collective-permute-done((bf16[512,2048]{1,0:T(8,128)(2,1)}, bf16[512,2048]{1,0:T(8,128)(2,1)}, u32[]{:S(2)}, u32[]{:S(2)}) %collective-permute-start.1) | collective-permute-done | bytes 2097184 | tf_op jit(solution)/shard_map/ppermute | solution.py:72
  110.2 3.1 constant_dynamic-update-slice_fusion.7
  113.3 3.1 constant_dynamic-update-slice_fusion.6
  117.8 33.6 %collective-permute-done.2 = bf16[512,2048]{1,0:T(8,128)(2,1)} collective-permute-done((bf16[512,2048]{1,0:T(8,128)(2,1)S(1)}, bf16[512,2048]{1,0:T(8,128)(2,1)}, u32[]{:S(2)}, u32[]{:S(2)}) %collective-permute-start.2) | collective-permute-done | bytes 2097184 | tf_op jit(solution)/shard_map/ppermute | solution.py:74
  151.4 3.1 constant_dynamic-update-slice_fusion.4
  154.5 3.1 constant_dynamic-update-slice_fusion.3
  157.6 3.1 constant_dynamic-update-slice_fusion.2
  162.1 3.2 constant_dynamic-update-slice_fusion
  165.4 16.2 %fusion.36 = (f32[512,1024]{1,0:T(8,128)}, bf16[512,1024]{1,0:T(8,128)(2,1)S(1)}, f32[512,1024]{1,0:T(8,128)}) fusion(bf16[512,1024]{1,0:T(8,128)(2,1)S(1)} %copy-done.4, bf16[8192,1024]{1,0:T(8,128)(2,1)} %all-gather.2.cloned.1.call-done, bf16[512,16384]{1,0:T(8,128)(2,1)} %constant_dynamic-update-slice_fusion, s32[]{:T(128)S(6)} %select_n.57), kind=kOutput, calls=%fused_computation.97 | convolution fusion | flops 8592031744 | bytes 31457284 | tf_op jit(solution)/shard_map/dot_general | solution.py:86
  187.5 58.3 %while.44 = (s32[]{:T(128)}, f32[512,1024]{1,0:T(8,128)S(1)}, f32[1024,128]{0,1:T(8,128)}, bf16[639,1024]{1,0:T(8,128)(2,1)S(1)}, s32[]{:T(128)}, /*index=5*/s32...) while((s32[]{:T(128)}, f32[512,1024]{1,0:T(8,128)S(1)}, ...), condition=%wide.region_3.4_spmd.clone, body=%wide.region_2.3_spmd.clone.sunk | while | flops 9444368 | bytes 24258916 | solution.py:38
  245.9 3.7 fusion.28
  250.6 6.5 collective-permute-start.3
  259.2 374.7 %while.42 = (s32[]{:T(128)}, f32[16,8,1024]{2,1,0:T(8,128)}, s32[16]{0:T(128)S(1)}, bf16[639,1024]{1,0:T(8,128)(2,1)S(1)}, f32[512,1024]{1,0:T(8,128)}, /*index=...) while((s32[]{:T(128)}, f32[16,8,1024]{2,1,0:T(8,128)}, s32[16]{0:T(128)S(1)}, ...), condition=%wide.region_6.7_spmd, body=%wide.region_4.6_spmd.sunk | while | flops 8911879 | bytes 55716028 | solution.py:61
  273.2 8.8 multiply_reduce_fusion.2
  296.7 8.8 multiply_reduce_fusion.2
  320.1 8.8 multiply_reduce_fusion.2
  343.5 8.8 multiply_reduce_fusion.2
  366.9 8.8 multiply_reduce_fusion.2
  390.3 8.8 multiply_reduce_fusion.2
  413.8 8.8 multiply_reduce_fusion.2
  437.2 8.8 multiply_reduce_fusion.2
  460.6 8.8 multiply_reduce_fusion.2
  484.0 8.8 multiply_reduce_fusion.2
  507.4 8.8 multiply_reduce_fusion.2
  530.8 8.8 multiply_reduce_fusion.2
  554.3 8.8 multiply_reduce_fusion.2
  577.7 8.8 multiply_reduce_fusion.2
  601.1 8.8 multiply_reduce_fusion.2
  624.5 8.8 multiply_reduce_fusion.2
  633.9 58.5 %while.43 = (s32[]{:T(128)}, f32[512,1024]{1,0:T(8,128)S(1)}, f32[1024,128]{0,1:T(8,128)}, bf16[639,1024]{1,0:T(8,128)(2,1)S(1)}, s32[]{:T(128)}, /*index=5*/s32...) while((s32[]{:T(128)}, f32[512,1024]{1,0:T(8,128)S(1)}, ...), condition=%wide.region_1.2_spmd.clone, body=%wide.region_0.1_spmd.clone.sunk | while | flops 9444370 | bytes 24258944 | solution.py:38
  635.4 2.2 fusion.57
  639.0 2.2 fusion.57
  642.6 2.2 fusion.57
  646.2 2.2 fusion.57
  650.0 2.2 fusion.57
  653.6 2.2 fusion.57
  657.4 2.2 fusion.57
  661.0 2.2 fusion.57
  671.9 2.2 fusion.57
  682.8 2.2 fusion.57
  686.5 2.2 fusion.57
  692.4 17.8 %fusion.24 = f32[8192,1024]{1,0:T(8,128)} fusion(bf16[512,16384]{1,0:T(8,128)(2,1)} %constant_dynamic-update-slice_fusion, s32[]{:T(128)S(6)} %select_n.57, f32[512,1024]{1,0:T(8,128)S(1)} %get-tuple-element.259, bf16[512,1024]{1,0:T(8,128)(2,1)} %param.12), kind=kOutput, calls=%fused_computation.69 | convolution fusion | flops 8591507456 | bytes 45088772 | tf_op jit(solution)/shard_map/dot_general | solution.py:101
  710.3 2.9 multiply_convert_fusion
  713.1 404.3 %all-reduce.3.cloned.1.call-done = (f32[1024,128]{0,1:T(8,128)}, f32[8192,1024]{1,0:T(8,128)}) async-done(((f32[1024,128]{0,1:T(8,128)}, f32[8192,1024]{1,0:T(8,128)}), (f32[1024,128]{0,1:T(8,128)}, f32[8192,1024]{1,0:T(8,128)})) %all-reduce.3.cloned.1.call-update) | async-done | bytes 34078736 | tf_op jit(solution)/shard_map/psum | solution.py:99
  1119.5 4.8 constant_dynamic-slice_fusion.16
  (293 shorter events, 329.6 us)
Async XLA Ops:
  7.2 1.6 copy-start
  7.2 158.2 %all-gather.2.cloned.1.call-start = ((), (), s32[]{:S(2)}) async-start(), calls=%async_computation | async-start | bytes 18874368 | tf_op jit(solution)/shard_map/all_gather | solution.py:88
  7.9 1109.5 %all-reduce.3.cloned.1.call-start = ((), (), s32[]{:S(2)}) async-start(), calls=%async_computation.1 | async-start | bytes 68157440 | tf_op jit(solution)/shard_map/psum | solution.py:99
  8.8 50.8 %collective-permute-start = (bf16[512,2048]{1,0:T(8,128)(2,1)S(1)}, bf16[512,2048]{1,0:T(8,128)(2,1)}, u32[]{:S(2)}, u32[]{:S(2)}) collective-permute-start(bf16[512,2048]{1,0:T(8,128)(2,1)S(1)} %copy-done), channel_id=1, source_target_pairs={{0,1},{1,2},{2,3},{3,0},{4,5},{5,6},{6,7},{7,4},{8,9},{9,10},{10,1... | collective-permute-start | bytes 6291464 | tf_op jit(solution)/shard_map/ppermute | solution.py:72
  59.5 50.7 %collective-permute-start.1 = (bf16[512,2048]{1,0:T(8,128)(2,1)}, bf16[512,2048]{1,0:T(8,128)(2,1)}, u32[]{:S(2)}, u32[]{:S(2)}) collective-permute-start(bf16[512,2048]{1,0:T(8,128)(2,1)} %collective-permute-done), channel_id=1, source_target_pairs={{0,1},{1,2},{2,3},{3,0},{4,5},{5,6},{6,7},{7,4},{8,9},{9,10},{10,1... | collective-permute-start | bytes 6291464 | tf_op jit(solution)/shard_map/ppermute | solution.py:72
  59.5 91.9 %collective-permute-start.2 = (bf16[512,2048]{1,0:T(8,128)(2,1)S(1)}, bf16[512,2048]{1,0:T(8,128)(2,1)}, u32[]{:S(2)}, u32[]{:S(2)}) collective-permute-start(bf16[512,2048]{1,0:T(8,128)(2,1)S(1)} %copy-done), channel_id=1, source_target_pairs={{0,3},{1,0},{2,1},{3,2},{4,7},{5,4},{6,5},{7,6},{8,11},{9,8},{10,9... | collective-permute-start | bytes 6291464 | tf_op jit(solution)/shard_map/ppermute | solution.py:74
  162.1 3.2 copy-start.4
  165.4 18.5 %copy-start.3 = (bf16[1024,128]{1,0:T(8,128)(2,1)S(1)}, bf16[1024,128]{1,0:T(8,128)(2,1)}, u32[]{:S(2)}) copy-start(bf16[1024,128]{1,0:T(8,128)(2,1)} %param.15) | copy-start | bytes 786436
  181.6 1.0 copy-start.2
  182.6 3.6 collective-permute-start.4
  249.6 1.0 copy-start.1
  250.6 7.0 collective-permute-start.3
Sparse Core Ops, SparseCore 0:
  9.9 92.5 all-gather.1
  710.4 406.9 all-reduce.2
